TPU v7x, 32 devices: a whole 2x2x4 slice. The times are simulated.
32 devices in a mesh: groups: 2 (over y), blk: 4 (over z), uly: 2 (over x), cfg: 2 (over core).
Axes of the slice: x: 2, y: 2, z: 4, core: 2. Of those that a mesh axis runs over, the one named last changes fastest.
Arguments:
- query_rows: bfloat16 [2, 1024, 1536], P('cfg', ('groups', 'blk', 'uly')), parts along dimension 1, may hold values from -6 to 6
- key_rows: bfloat16 [2, 1024, 1536], P('cfg', ('groups', 'blk', 'uly')), parts along dimension 1, may hold values from -6 to 6
- value_rows: bfloat16 [2, 1024, 1536], P('cfg', ('groups', 'blk', 'uly')), parts along dimension 1, may hold values from -6 to 6
Outputs:
- attended: bfloat16 [2, 1024, 1536], P('cfg', ('groups', 'blk', 'uly')), parts along dimension 1
There are 2 independent parts, one for each index of `groups`. A program takes and returns all parts, laid end to end along the dimension named above; each array names one. Nothing has to cross between parts.
All inputs are finite; a program needn't handle non-finite values.
Results may differ from a plain program's by a relative error of at most 0.0045.
Values may be sent and summed in bfloat16 or wider, within the bound.
A program may use at most 128 MiB of HBM per device.

v0:
```python
import math
import jax
import jax.numpy as jnp
from jax import lax
from jax.sharding import PartitionSpec as P

HD = 128


def attend(queries, key_part, value_part):
    query_mat = queries[0, :, 0]
    row_count, head_count, head_size = query_mat.shape
    score_scale = 1.0 / math.sqrt(head_size)
    start_state = (
        jnp.full((head_count, row_count), -1e30, jnp.float32),
        jnp.zeros((head_count, row_count), jnp.float32),
        jnp.zeros((row_count, head_count, head_size), jnp.float32),
    )

    def absorb(state, pieces):
        key_piece = pieces[0][0, :, 0]
        value_piece = pieces[1][0, :, 0]
        scores = (
            jnp.einsum("qhd,khd->hqk", query_mat, key_piece, preferred_element_type=jnp.float32)
            * score_scale
        )
        running, totals, accumulated = state
        new_max = jnp.maximum(running, jnp.max(scores, axis=2))
        weights = jnp.exp(scores - new_max[:, :, None])
        factor = jnp.exp(running - new_max)
        totals = totals * factor + jnp.sum(weights, axis=2)
        probabilities = weights.astype(jnp.bfloat16)
        contrib = jnp.einsum(
            "hqk,khd->qhd", probabilities, value_piece, preferred_element_type=jnp.float32
        )
        accumulated = accumulated * factor.T[:, :, None] + contrib
        return (new_max, totals, accumulated)

    whole_keys, whole_values = (
        lax.all_gather(key_part, "blk", axis=1, tiled=True),
        lax.all_gather(value_part, "blk", axis=1, tiled=True),
    )
    key_count = whole_keys.shape[1]
    block_rows = math.gcd(key_count, 1024)

    def one_block(state, counter):
        offset = counter * block_rows
        key_block = lax.dynamic_slice_in_dim(whole_keys, offset, block_rows, 1)
        value_block = lax.dynamic_slice_in_dim(whole_values, offset, block_rows, 1)
        return (absorb(state, (key_block, value_block)), None)

    result, unused = lax.scan(
        one_block, start_state, jnp.arange(key_count // block_rows, dtype=jnp.int32)
    )
    output = (result[2] / result[1].T[:, :, None]).astype(jnp.bfloat16)
    return output.reshape(1, row_count, 1, head_count, head_size)


def regroup_back(attended_part):
    return lax.all_to_all(attended_part, "uly", split_axis=1, concat_axis=2, tiled=True)


def whole_pass(triple):
    return regroup_back(attend(triple[0], triple[1], triple[2]))


def local(query_rows, key_rows, value_rows):
    ulysses = lax.axis_size("uly")
    tokens = query_rows.shape[1]
    width = query_rows.shape[2]
    heads_local = width // HD // ulysses

    def split_heads(array):
        return array.reshape(1, tokens, ulysses, heads_local, HD)

    sectioned = (split_heads(query_rows), split_heads(key_rows), split_heads(value_rows))
    moved = (
        lax.all_to_all(sectioned[0], "uly", split_axis=2, concat_axis=1, tiled=True),
        lax.all_to_all(sectioned[1], "uly", split_axis=2, concat_axis=1, tiled=True),
        lax.all_to_all(sectioned[2], "uly", split_axis=2, concat_axis=1, tiled=True),
    )
    merged = whole_pass(moved)
    return merged.reshape(1, tokens, width)


def solution(mesh):
    in_specs = (
        P("cfg", ("groups", "blk", "uly"), None),
        P("cfg", ("groups", "blk", "uly"), None),
        P("cfg", ("groups", "blk", "uly"), None),
    )
    out_specs = P("cfg", ("groups", "blk", "uly"), None)
    return jax.shard_map(local, mesh=mesh, in_specs=in_specs, out_specs=out_specs, check_vma=False)
```

profile of v0, /device:TPU:0, one launch (start us, length us, event | category | flops | bytes accessed | tf_op | source)
XLA Modules:
  0.0 69.2 jit_solution(18183577460159070147)
XLA Ops:
  0.0 0.0 copy-start
  0.0 1.2 %reshape.23 = bf16[1,64,2,6,128]{4,3,2,1,0:T(8,128)(2,1)S(1)} reshape(bf16[1,64,1536]{2,1,0:T(8,128)(2,1)} %param.4) | data formatting | bytes 393216 | tf_op jit(solution)/shard_map/reshape | solution.py:74
  1.2 0.7 %copy.14 = bf16[1,64,2,6,128]{4,1,3,0,2:T(8,128)(2,1)} copy(bf16[1,64,2,6,128]{4,3,2,1,0:T(8,128)(2,1)S(1)} %reshape.23) | data formatting | bytes 393216 | tf_op jit(solution)/shard_map/reshape | solution.py:74
  1.9 4.2 %all-to-all-start.1 = ((bf16[1,64,2,6,128]{4,1,3,0,2:T(8,128)(2,1)}), bf16[1,64,2,6,128]{4,1,3,0,2:T(8,128)(2,1)S(1)}, u32[]{:S(2)}, u32[]{:S(2)}) async-start(bf16[1,64,2,6,128]{4,1,3,0,2:T(8,128)(2,1)} %copy.14), calls=%async_computation.1 | async-start | bytes 393216 | tf_op jit(solution)/shard_map/all_to_all | solution.py:79
  6.2 1.2 %reshape.22 = bf16[1,64,2,6,128]{4,3,2,1,0:T(8,128)(2,1)S(1)} reshape(bf16[1,64,1536]{2,1,0:T(8,128)(2,1)} %param.3) | data formatting | bytes 393216 | tf_op jit(solution)/shard_map/reshape | solution.py:74
  7.3 0.7 %copy.12 = bf16[1,64,2,6,128]{4,1,3,0,2:T(8,128)(2,1)} copy(bf16[1,64,2,6,128]{4,3,2,1,0:T(8,128)(2,1)S(1)} %reshape.22) | data formatting | bytes 393216 | tf_op jit(solution)/shard_map/reshape | solution.py:74
  8.1 0.0 copy-done
  8.1 0.2 reshape.24
  8.3 0.7 %copy.16 = bf16[1,64,2,6,128]{4,1,3,0,2:T(8,128)(2,1)} copy(bf16[1,64,2,6,128]{4,3,2,1,0:T(8,128)(2,1)S(1)} %reshape.24) | data formatting | bytes 393216 | tf_op jit(solution)/shard_map/reshape | solution.py:74
  9.0 2.3 %all-to-all-done.1 = bf16[1,64,2,6,128]{4,1,3,0,2:T(8,128)(2,1)S(1)} async-done(((bf16[1,64,2,6,128]{4,1,3,0,2:T(8,128)(2,1)}), bf16[1,64,2,6,128]{4,1,3,0,2:T(8,128)(2,1)S(1)}, u32[]{:S(2)}, u32[]{:S(2)}) %all-to-all-start.1) | async-done | bytes 196640 | tf_op jit(solution)/shard_map/all_to_all | solution.py:79
  11.3 3.4 %all-to-all-start = ((bf16[1,64,2,6,128]{4,1,3,0,2:T(8,128)(2,1)}), bf16[1,64,2,6,128]{4,1,3,0,2:T(8,128)(2,1)S(1)}, u32[]{:S(2)}, u32[]{:S(2)}) async-start(bf16[1,64,2,6,128]{4,1,3,0,2:T(8,128)(2,1)} %copy.12), calls=%async_computation | async-start | bytes 393216 | tf_op jit(solution)/shard_map/all_to_all | solution.py:78
  14.8 20.0 %all_gather.6 = bf16[1,512,1,6,128]{4,1,3,2,0:T(8,128)(2,1)S(1)} all-gather(bf16[1,128,1,6,128]{4,1,3,2,0:T(8,128)(2,1)S(1)} %bitcast.51), channel_id=1, replica_groups=mesh['groups'=2,'blk'=4,'uly'=2,'cfg'=2] {'blk'}, dimensions={1}, use_global_device_ids=true | all-gather | bytes 983040 | tf_op jit(solution)/shard_map/all_gather | solution.py:40
  34.8 0.0 all-to-all-done
  34.8 3.4 %all-to-all-start.2 = ((bf16[1,64,2,6,128]{4,1,3,0,2:T(8,128)(2,1)}), bf16[1,64,2,6,128]{4,1,3,0,2:T(8,128)(2,1)S(1)}, u32[]{:S(2)}, u32[]{:S(2)}) async-start(bf16[1,64,2,6,128]{4,1,3,0,2:T(8,128)(2,1)} %copy.16), calls=%async_computation.2 | async-start | bytes 393216 | tf_op jit(solution)/shard_map/all_to_all | solution.py:80
  38.2 0.4 fusion.10
  38.7 0.5 fusion
  39.2 3.8 %all-to-all-done.2 = bf16[1,64,2,6,128]{4,1,3,0,2:T(8,128)(2,1)S(1)} async-done(((bf16[1,64,2,6,128]{4,1,3,0,2:T(8,128)(2,1)}), bf16[1,64,2,6,128]{4,1,3,0,2:T(8,128)(2,1)S(1)}, u32[]{:S(2)}, u32[]{:S(2)}) %all-to-all-start.2) | async-done | bytes 196640 | tf_op jit(solution)/shard_map/all_to_all | solution.py:80
  43.0 17.0 %all_gather.7 = bf16[1,512,1,6,128]{4,1,3,2,0:T(8,128)(2,1)S(1)} all-gather(bf16[1,128,1,6,128]{4,1,3,2,0:T(8,128)(2,1)S(1)} %bitcast.52), channel_id=1, replica_groups=mesh['groups'=2,'blk'=4,'uly'=2,'cfg'=2] {'blk'}, dimensions={1}, use_global_device_ids=true | all-gather | bytes 983040 | tf_op jit(solution)/shard_map/all_gather | solution.py:41
  60.0 0.5 fusion.5
  60.6 0.1 copy.18
  60.7 7.6 %all_to_all.66 = bf16[1,128,1,6,128]{4,3,2,0,1:T(8,128)(2,1)S(1)} all-to-all(bf16[1,128,1,6,128]{4,3,2,0,1:T(8,128)(2,1)S(1)} %copy.18), channel_id=1, replica_groups=mesh['groups'=2,'blk'=4,'uly'=2,'cfg'=2] {'uly'}, dimensions={1} | all-to-all | bytes 393216 | tf_op jit(solution)/shard_map/all_to_all | solution.py:60
  68.3 0.9 %reshape.26 = bf16[1,64,1536]{2,1,0:T(8,128)(2,1)} reshape(bf16[1,64,2,1,6,128]{5,4,2,1,3,0:T(8,128)(2,1)S(1)} %bitcast.45) | data formatting | bytes 393216 | tf_op jit(solution)/shard_map/reshape | solution.py:83
  (6 shorter events, 0.1 us)
Async XLA Ops:
  0.0 8.1 %copy-start = (bf16[1,64,1536]{2,1,0:T(8,128)(2,1)S(1)}, bf16[1,64,1536]{2,1,0:T(8,128)(2,1)}, u32[]{:S(2)}) copy-start(bf16[1,64,1536]{2,1,0:T(8,128)(2,1)} %param.5) | copy-start | bytes 589828
  1.9 9.4 %all-to-all-start.1 = ((bf16[1,64,2,6,128]{4,1,3,0,2:T(8,128)(2,1)}), bf16[1,64,2,6,128]{4,1,3,0,2:T(8,128)(2,1)S(1)}, u32[]{:S(2)}, u32[]{:S(2)}) async-start(bf16[1,64,2,6,128]{4,1,3,0,2:T(8,128)(2,1)} %copy.14), calls=%async_computation.1 | async-start | bytes 393216 | tf_op jit(solution)/shard_map/all_to_all | solution.py:79
  11.3 23.5 %all-to-all-start = ((bf16[1,64,2,6,128]{4,1,3,0,2:T(8,128)(2,1)}), bf16[1,64,2,6,128]{4,1,3,0,2:T(8,128)(2,1)S(1)}, u32[]{:S(2)}, u32[]{:S(2)}) async-start(bf16[1,64,2,6,128]{4,1,3,0,2:T(8,128)(2,1)} %copy.12), calls=%async_computation | async-start | bytes 393216 | tf_op jit(solution)/shard_map/all_to_all | solution.py:78
  34.8 8.2 %all-to-all-start.2 = ((bf16[1,64,2,6,128]{4,1,3,0,2:T(8,128)(2,1)}), bf16[1,64,2,6,128]{4,1,3,0,2:T(8,128)(2,1)S(1)}, u32[]{:S(2)}, u32[]{:S(2)}) async-start(bf16[1,64,2,6,128]{4,1,3,0,2:T(8,128)(2,1)} %copy.16), calls=%async_computation.2 | async-start | bytes 393216 | tf_op jit(solution)/shard_map/all_to_all | solution.py:80
where the time goes:
time: 69.6 us; the launch traced here: 69.2 us
  blocking collectives  44.5 us (64%)
  starting transfers between devices  11.1 us (16%)
  waiting for transfers between devices  6.09 us (9%)
  local copies, waits for them, and re-layouts  5.94 us (9%)
  matrix products  0.98 us (1%)
    all_gather x1, blocking collectives, attend(): lax.all_gather(key_part, 'blk', axis=1, tiled=True)  20 us
    all_gather x1, blocking collectives, attend(): lax.all_gather(value_part, 'blk', axis=1, tiled=True)  17 us
    all_to_all x1, blocking collectives, regroup_back(): lax.all_to_all(attended_part, 'uly', split_axis=1, concat_axis=2, tiled=T...  7.56 us
    reshape x6, local copies, waits for them, and re-layouts, split_heads(): return array.reshape(1, tokens, ulysses, heads_local, HD)  4.8 us
    all_to_all x1, starting transfers between devices, local(): lax.all_to_all(sectioned[1], 'uly', split_axis=2, concat_axis=1, tiled=True)  4.23 us
    all_to_all x1, waiting for transfers between devices, local(): lax.all_to_all(sectioned[2], 'uly', split_axis=2, concat_axis=1, tiled=True)  3.81 us
    all_to_all x1, starting transfers between devices, local(): lax.all_to_all(sectioned[2], 'uly', split_axis=2, concat_axis=1, tiled=True)  3.43 us
    all_to_all x1, starting transfers between devices, local(): lax.all_to_all(sectioned[0], 'uly', split_axis=2, concat_axis=1, tiled=True)  3.43 us
  transfers between devices with their start and end apart: 3, of which 2 were waited for; matrix products, arithmetic and copies ran while one was open for 6% of the time, Pallas kernels for 0%

commit v1 on v0

--- a/solution.py
+++ b/solution.py
@@ -5,6 +5,27 @@
 from jax.sharding import PartitionSpec as P
 
 HD = 128
+
+
+def collect(shard, axis, dim):
+    devices, index, rows = (lax.axis_size(axis), lax.axis_index(axis), shard.shape[dim])
+    right = [(i, (i + 1) % devices) for i in range(devices)]
+    behind = [(i, (i - 1) % devices) for i in range(devices)]
+    filled = jnp.zeros((*shard.shape[:dim], devices * rows, *shard.shape[dim + 1 :]), shard.dtype)
+    filled = lax.dynamic_update_slice_in_dim(filled, shard, index * rows, axis=dim)
+    from_left = from_right = shard
+    halfway = devices // 2
+    for lap in range(1, halfway + 1):
+        from_left = lax.ppermute(from_left, axis, right)
+        filled = lax.dynamic_update_slice_in_dim(
+            filled, from_left, (index - lap) % devices * rows, axis=dim
+        )
+        if lap < devices - halfway:
+            from_right = lax.ppermute(from_right, axis, behind)
+            filled = lax.dynamic_update_slice_in_dim(
+                filled, from_right, (index + lap) % devices * rows, axis=dim
+            )
+    return filled
 
 
 def attend(queries, key_part, value_part):
@@ -38,7 +59,7 @@
 
     whole_keys, whole_values = (
         lax.all_gather(key_part, "blk", axis=1, tiled=True),
-        lax.all_gather(value_part, "blk", axis=1, tiled=True),
+        collect(value_part, "blk", 1),
     )
     key_count = whole_keys.shape[1]
     block_rows = math.gcd(key_count, 1024)

time: 69.6 us -> 64.3 us (0.924)
  blocking collectives: 44.5 us -> 27.3 us
  waiting for transfers between devices: 6.09 us -> 10.7 us
  starting transfers between devices: 11.1 us -> 15.3 us
  local copies, waits for them, and re-layouts: 5.94 us -> 8.92 us
    all_gather x1 -> x0, blocking collectives: 17 us -> none  [attend(): lax.all_gather(value_part, 'blk', axis=1, tiled=True)]
    ppermute x0 -> x3, waiting for transfers between devices: none -> 7.44 us  [the longest x2 7.44 us: collect(): from_left = lax.ppermute(from_left, axis, right)]
    ppermute x0 -> x3, starting transfers between devices: none -> 4.24 us  [the longest x2 2.14 us: collect(): from_left = lax.ppermute(from_left, axis, right)]
    squeeze x0 -> x5, local copies, waits for them, and re-layouts: none -> 2.59 us  [absorb(): value_piece = pieces[1][0, :, 0]]
    all_to_all x1, waiting for transfers between devices: 2.28 us -> 0.01 us  [local(): lax.all_to_all(sectioned[1], 'uly', split_axis=2, concat_axis=1, tiled=True)]
    all_to_all x1, starting transfers between devices: 4.23 us -> 3.43 us  [local(): lax.all_to_all(sectioned[1], 'uly', split_axis=2, concat_axis=1, tiled=True)]
    all_to_all x1, starting transfers between devices: 3.43 us -> 4.23 us  [local(): lax.all_to_all(sectioned[2], 'uly', split_axis=2, concat_axis=1, tiled=True)]
  transfers between devices with their start and end apart: 3 -> 6, of which waited for: 2 -> 2; matrix products, arithmetic and copies ran while one was open for 6% -> 8% of each run, Pallas kernels for 0% -> 0%
where the time goes in v1:
time: 64.3 us; the launch traced here: 63.9 us
  blocking collectives  27.3 us (42%)
  starting transfers between devices  15.3 us (24%)
  waiting for transfers between devices  10.7 us (17%)
  local copies, waits for them, and re-layouts  8.92 us (14%)
  matrix products  0.91 us (1%)
    all_gather x1, blocking collectives, attend(): lax.all_gather(key_part, 'blk', axis=1, tiled=True)  19.3 us
    all_to_all x1, blocking collectives, regroup_back(): lax.all_to_all(attended_part, 'uly', split_axis=1, concat_axis=2, tiled=T...  7.97 us
    ppermute x2, waiting for transfers between devices, collect(): from_left = lax.ppermute(from_left, axis, right)  7.44 us
    reshape x6, local copies, waits for them, and re-layouts, split_heads(): return array.reshape(1, tokens, ulysses, heads_local, HD)  4.81 us
    all_to_all x1, starting transfers between devices, local(): lax.all_to_all(sectioned[2], 'uly', split_axis=2, concat_axis=1, tiled=True)  4.23 us
    all_to_all x1, starting transfers between devices, local(): lax.all_to_all(sectioned[0], 'uly', split_axis=2, concat_axis=1, tiled=True)  3.43 us
    all_to_all x1, starting transfers between devices, local(): lax.all_to_all(sectioned[1], 'uly', split_axis=2, concat_axis=1, tiled=True)  3.43 us
    all_to_all x1, waiting for transfers between devices, local(): lax.all_to_all(sectioned[2], 'uly', split_axis=2, concat_axis=1, tiled=True)  3.25 us
  transfers between devices with their start and end apart: 6, of which 2 were waited for; matrix products, arithmetic and copies ran while one was open for 8% of the time, Pallas kernels for 0%

profile of v1, /device:TPU:0, one launch (start us, length us, event | category | flops | bytes accessed | tf_op | source)
XLA Modules:
  0.0 63.9 jit_solution(4928422299912232916)
XLA Ops:
  0.0 1.2 %reshape.33 = bf16[1,64,2,6,128]{4,3,2,1,0:T(8,128)(2,1)S(1)} reshape(bf16[1,64,1536]{2,1,0:T(8,128)(2,1)} %param.5) | data formatting | bytes 393216 | tf_op jit(solution)/shard_map/reshape | solution.py:95
  1.2 0.7 %copy.23 = bf16[1,64,2,6,128]{4,1,3,0,2:T(8,128)(2,1)} copy(bf16[1,64,2,6,128]{4,3,2,1,0:T(8,128)(2,1)S(1)} %reshape.33) | data formatting | bytes 393216 | tf_op jit(solution)/shard_map/reshape | solution.py:95
  1.9 4.2 %all-to-all-start.2 = ((bf16[1,64,2,6,128]{4,1,3,0,2:T(8,128)(2,1)}), bf16[1,64,2,6,128]{4,1,3,0,2:T(8,128)(2,1)S(1)}, u32[]{:S(2)}, u32[]{:S(2)}) async-start(bf16[1,64,2,6,128]{4,1,3,0,2:T(8,128)(2,1)} %copy.23), calls=%async_computation.2 | async-start | bytes 393216 | tf_op jit(solution)/shard_map/all_to_all | solution.py:101
  6.2 1.2 %reshape.32 = bf16[1,64,2,6,128]{4,3,2,1,0:T(8,128)(2,1)S(1)} reshape(bf16[1,64,1536]{2,1,0:T(8,128)(2,1)} %param.4) | data formatting | bytes 393216 | tf_op jit(solution)/shard_map/reshape | solution.py:95
  7.3 0.7 %copy.21 = bf16[1,64,2,6,128]{4,1,3,0,2:T(8,128)(2,1)} copy(bf16[1,64,2,6,128]{4,3,2,1,0:T(8,128)(2,1)S(1)} %reshape.32) | data formatting | bytes 393216 | tf_op jit(solution)/shard_map/reshape | solution.py:95
  8.1 3.2 %all-to-all-done.2 = bf16[1,64,2,6,128]{4,1,3,0,2:T(8,128)(2,1)S(1)} async-done(((bf16[1,64,2,6,128]{4,1,3,0,2:T(8,128)(2,1)}), bf16[1,64,2,6,128]{4,1,3,0,2:T(8,128)(2,1)S(1)}, u32[]{:S(2)}, u32[]{:S(2)}) %all-to-all-start.2) | async-done | bytes 196640 | tf_op jit(solution)/shard_map/all_to_all | solution.py:101
  11.3 3.4 %all-to-all-start.1 = ((bf16[1,64,2,6,128]{4,1,3,0,2:T(8,128)(2,1)}), bf16[1,64,2,6,128]{4,1,3,0,2:T(8,128)(2,1)S(1)}, u32[]{:S(2)}, u32[]{:S(2)}) async-start(bf16[1,64,2,6,128]{4,1,3,0,2:T(8,128)(2,1)} %copy.21), calls=%async_computation.1 | async-start | bytes 393216 | tf_op jit(solution)/shard_map/all_to_all | solution.py:100
  14.8 0.2 reshape.31
  15.1 0.7 %copy.19 = bf16[1,64,2,6,128]{4,1,3,0,2:T(8,128)(2,1)} copy(bf16[1,64,2,6,128]{4,3,2,1,0:T(8,128)(2,1)S(1)} %reshape.31) | data formatting | bytes 393216 | tf_op jit(solution)/shard_map/reshape | solution.py:95
  15.8 2.0 %collective-permute-start = (bf16[1,128,1,6,128]{4,1,3,2,0:T(8,128)(2,1)S(1)}, bf16[1,128,1,6,128]{4,1,3,2,0:T(8,128)(2,1)}, u32[]{:S(2)}, u32[]{:S(2)}) collective-permute-start(bf16[1,128,1,6,128]{4,1,3,2,0:T(8,128)(2,1)S(1)} %bitcast.51), channel_id=1, source_target_pairs={{0,4},{4,8},{8,12},{12,0},{1,5},{5,9},{9,13},{13,1},{2,6},{6,10},{... | collective-permute-start | bytes 589832 | tf_op jit(solution)/shard_map/ppermute | solution.py:19
  17.8 2.1 %collective-permute-start.1 = (bf16[1,128,1,6,128]{4,1,3,2,0:T(8,128)(2,1)S(1)}, bf16[1,128,1,6,128]{4,1,3,2,0:T(8,128)(2,1)}, u32[]{:S(2)}, u32[]{:S(2)}) collective-permute-start(bf16[1,128,1,6,128]{4,1,3,2,0:T(8,128)(2,1)S(1)} %bitcast.52), channel_id=1, source_target_pairs={{0,12},{4,0},{8,4},{12,8},{1,13},{5,1},{9,5},{13,9},{2,14},{6,2},{... | collective-permute-start | bytes 589832 | tf_op jit(solution)/shard_map/ppermute | solution.py:24
  19.9 0.0 all-to-all-done.1
  19.9 3.4 %all-to-all-start = ((bf16[1,64,2,6,128]{4,1,3,0,2:T(8,128)(2,1)}), bf16[1,64,2,6,128]{4,1,3,0,2:T(8,128)(2,1)S(1)}, u32[]{:S(2)}, u32[]{:S(2)}) async-start(bf16[1,64,2,6,128]{4,1,3,0,2:T(8,128)(2,1)} %copy.19), calls=%async_computation | async-start | bytes 393216 | tf_op jit(solution)/shard_map/all_to_all | solution.py:99
  23.4 19.3 %all_gather.3 = bf16[1,512,1,6,128]{4,1,3,2,0:T(8,128)(2,1)S(1)} all-gather(bf16[1,128,1,6,128]{4,1,3,2,0:T(8,128)(2,1)S(1)} %bitcast.55), channel_id=1, replica_groups=mesh['groups'=2,'blk'=4,'uly'=2,'cfg'=2] {'blk'}, dimensions={1}, use_global_device_ids=true | all-gather | bytes 983040 | tf_op jit(solution)/shard_map/all_gather | solution.py:61
  42.7 0.2 copy.25
  42.9 0.0 all-to-all-done
  42.9 0.4 fusion.9
  43.4 0.5 fusion
  43.9 0.1 squeeze.24
  43.9 0.1 constant_dynamic-update-slice_fusion.3
  44.0 1.1 %copy.26 = bf16[128,6,128]{0,2,1:T(8,128)(2,1)S(1)} copy(bf16[128,6,128]{2,0,1:T(8,128)(2,1)} %bitcast.13) | data formatting | bytes 393216 | tf_op jit(solution)/shard_map/while/body/eval_jaxpr/squeeze | solution.py:43
  45.1 1.1 %copy.27 = bf16[128,6,128]{0,2,1:T(8,128)(2,1)S(1)} copy(bf16[128,6,128]{2,0,1:T(8,128)(2,1)} %bitcast.15) | data formatting | bytes 393216 | tf_op jit(solution)/shard_map/while/body/eval_jaxpr/squeeze | solution.py:43
  46.2 0.2 collective-permute-start.2
  46.5 0.1 constant_dynamic-update-slice_fusion.1
  46.5 7.4 %collective-permute-done.2 = bf16[1,128,1,6,128]{4,1,3,2,0:T(8,128)(2,1)S(1)} collective-permute-done((bf16[1,128,1,6,128]{4,1,3,2,0:T(8,128)(2,1)}, bf16[1,128,1,6,128]{4,1,3,2,0:T(8,128)(2,1)S(1)}, u32[]{:S(2)}, u32[]{:S(2)}) %collective-permute-start.2) | collective-permute-done | bytes 196640 | tf_op jit(solution)/shard_map/ppermute | solution.py:19
  53.9 0.2 copy.28
  54.1 0.1 constant_dynamic-update-slice_fusion
  54.2 0.5 fusion.5
  54.6 0.2 copy.29
  54.8 8.0 %all_to_all.66 = bf16[1,128,1,6,128]{4,3,2,0,1:T(8,128)(2,1)S(1)} all-to-all(bf16[1,128,1,6,128]{4,3,2,0,1:T(8,128)(2,1)S(1)} %copy.29), channel_id=1, replica_groups=mesh['groups'=2,'blk'=4,'uly'=2,'cfg'=2] {'uly'}, dimensions={1} | all-to-all | bytes 393216 | tf_op jit(solution)/shard_map/all_to_all | solution.py:81
  62.8 0.1 copy.31
  63.0 0.9 %reshape.35 = bf16[1,64,1536]{2,1,0:T(8,128)(2,1)} reshape(bf16[1,64,2,1,6,128]{5,4,2,1,3,0:T(8,128)(2,1)S(1)} %copy.31) | data formatting | bytes 393216 | tf_op jit(solution)/shard_map/reshape | solution.py:104
  (11 shorter events, 0.1 us)
Async XLA Ops:
  0.0 14.8 %copy-start = (bf16[1,64,1536]{2,1,0:T(8,128)(2,1)S(1)}, bf16[1,64,1536]{2,1,0:T(8,128)(2,1)}, u32[]{:S(2)}) copy-start(bf16[1,64,1536]{2,1,0:T(8,128)(2,1)} %param.3) | copy-start | bytes 589828
  1.9 9.4 %all-to-all-start.2 = ((bf16[1,64,2,6,128]{4,1,3,0,2:T(8,128)(2,1)}), bf16[1,64,2,6,128]{4,1,3,0,2:T(8,128)(2,1)S(1)}, u32[]{:S(2)}, u32[]{:S(2)}) async-start(bf16[1,64,2,6,128]{4,1,3,0,2:T(8,128)(2,1)} %copy.23), calls=%async_computation.2 | async-start | bytes 393216 | tf_op jit(solution)/shard_map/all_to_all | solution.py:101
  11.3 8.6 %all-to-all-start.1 = ((bf16[1,64,2,6,128]{4,1,3,0,2:T(8,128)(2,1)}), bf16[1,64,2,6,128]{4,1,3,0,2:T(8,128)(2,1)S(1)}, u32[]{:S(2)}, u32[]{:S(2)}) async-start(bf16[1,64,2,6,128]{4,1,3,0,2:T(8,128)(2,1)} %copy.21), calls=%async_computation.1 | async-start | bytes 393216 | tf_op jit(solution)/shard_map/all_to_all | solution.py:100
  15.8 28.2 %collective-permute-start = (bf16[1,128,1,6,128]{4,1,3,2,0:T(8,128)(2,1)S(1)}, bf16[1,128,1,6,128]{4,1,3,2,0:T(8,128)(2,1)}, u32[]{:S(2)}, u32[]{:S(2)}) collective-permute-start(bf16[1,128,1,6,128]{4,1,3,2,0:T(8,128)(2,1)S(1)} %bitcast.51), channel_id=1, source_target_pairs={{0,4},{4,8},{8,12},{12,0},{1,5},{5,9},{9,13},{13,1},{2,6},{6,10},{... | collective-permute-start | bytes 589832 | tf_op jit(solution)/shard_map/ppermute | solution.py:19
  17.8 27.3 %collective-permute-start.1 = (bf16[1,128,1,6,128]{4,1,3,2,0:T(8,128)(2,1)S(1)}, bf16[1,128,1,6,128]{4,1,3,2,0:T(8,128)(2,1)}, u32[]{:S(2)}, u32[]{:S(2)}) collective-permute-start(bf16[1,128,1,6,128]{4,1,3,2,0:T(8,128)(2,1)S(1)} %bitcast.52), channel_id=1, source_target_pairs={{0,12},{4,0},{8,4},{12,8},{1,13},{5,1},{9,5},{13,9},{2,14},{6,2},{... | collective-permute-start | bytes 589832 | tf_op jit(solution)/shard_map/ppermute | solution.py:24
  19.9 23.0 %all-to-all-start = ((bf16[1,64,2,6,128]{4,1,3,0,2:T(8,128)(2,1)}), bf16[1,64,2,6,128]{4,1,3,0,2:T(8,128)(2,1)S(1)}, u32[]{:S(2)}, u32[]{:S(2)}) async-start(bf16[1,64,2,6,128]{4,1,3,0,2:T(8,128)(2,1)} %copy.19), calls=%async_computation | async-start | bytes 393216 | tf_op jit(solution)/shard_map/all_to_all | solution.py:99
  46.2 7.7 %collective-permute-start.2 = (bf16[1,128,1,6,128]{4,1,3,2,0:T(8,128)(2,1)}, bf16[1,128,1,6,128]{4,1,3,2,0:T(8,128)(2,1)S(1)}, u32[]{:S(2)}, u32[]{:S(2)}) collective-permute-start(bf16[1,128,1,6,128]{4,1,3,2,0:T(8,128)(2,1)} %collective-permute-done), channel_id=1, source_target_pairs={{0,4},{4,8},{8,12},{12,0},{1,5},{5,9},{9,13},{13,1},{2,6},{6,10},{... | collective-permute-start | bytes 589832 | tf_op jit(solution)/shard_map/ppermute | solution.py:19
